TPU v7x, 128 devices: a whole 4x4x4 slice. The times are simulated.
128 devices in a mesh: row: 8 (over x, core), col: 16 (over y, z).
Axes of the slice: x: 4, y: 4, z: 4, core: 2. Of those that a mesh axis runs over, the one named last changes fastest.
Arguments:
- parent_front: float32 [16384, 16384], P('row', 'col'), as said below
- child_panels: float32 [8, 4096, 512], P('row', 'col'), may hold values from -6 to 6
- child_inverses: float32 [8, 512, 512], P('row'), as said below
- parent_index: int32 [8, 16], replicated, may hold values from 2 to 63, as said below
Outputs:
- panel: float32 [16384, 512], P('row')
- schur: float32 [16384, 16384], P('row', 'col')
Inputs may be any that keep to these rules, and one draw needn't show every extreme that they name: `parent_index`: entry (g, u) names the parent tile that receives tile row and tile column u of child g's update. Seen in blocks of 4 consecutive tiles, each child names every block exactly once, and at a given u the children name different blocks. No entry names one of the first 2 tiles. `parent_front`: Symmetric. In its leading 2 * 256 rows and columns, each diagonal entry is positive and exceeds the sum of magnitudes of the other entries of its row within that block. `child_inverses`: each matrix is lower triangular with a positive diagonal.
All inputs are finite; a program needn't handle non-finite values.
Results may differ from a plain program's by a relative error of at most 0.0003.
Values sent between devices are 32-bit elements; how exact they have to be, the bound alone decides.
A program may use at most 128 MiB of HBM per device.

v0:
```python
import jax
import jax.numpy as jnp
from jax import lax
from jax.sharding import PartitionSpec as P

TILE = 256
PCT = 4
NSP = 2


def from_root(block, axis, holder):
    block = jnp.where(lax.axis_index(axis) == holder, block, jnp.zeros_like(block))
    return lax.psum(block, axis)


def product(matrix_a, matrix_b):
    return jnp.dot(
        matrix_a, matrix_b, precision=lax.Precision.HIGHEST, preferred_element_type=jnp.float32
    )


def product_rows(matrix_a, matrix_b):
    return lax.dot_general(
        matrix_a,
        matrix_b,
        (((1,), (1,)), ((), ())),
        precision=lax.Precision.HIGHEST,
        preferred_element_type=jnp.float32,
    )


def place_tiles(received, row_tiles, col_tiles, live_mask, tile_count):
    target = row_tiles * PCT + col_tiles
    onehot = (target[None, :] == jnp.arange(tile_count)[:, None]).astype(jnp.float32) * live_mask[
        None, :
    ]
    flat_tiles = received.reshape(received.shape[0], TILE * TILE)
    return product(onehot, flat_tiles)


def per_device(parent_front, child_panels, child_inverses, parent_index):
    row_devices = lax.axis_size("row")
    col_devices = lax.axis_size("col")
    here_row = lax.axis_index("row")
    here_col = lax.axis_index("col")
    per_block = col_devices // row_devices
    row_count = PCT * per_block
    tile_count = row_count * PCT
    own_factor = product_rows(child_panels[0], child_inverses[0])
    my_list = lax.dynamic_index_in_dim(parent_index, here_row, 0, keepdims=False)
    block_of = parent_index // PCT
    update_col = product_rows(lax.all_gather(own_factor, "col", axis=0, tiled=True), own_factor)
    dest_row = my_list // PCT // per_block
    tile_ids = jnp.arange(col_devices, dtype=jnp.int32)
    same_dest = (dest_row[None, :] == dest_row[:, None]) & (tile_ids[None, :] < tile_ids[:, None])
    slot_index = jnp.sum(same_dest.astype(jnp.int32), axis=1)
    position = dest_row * per_block + slot_index
    send_order = jnp.zeros((col_devices,), jnp.int32).at[position].set(tile_ids)
    outgoing = update_col.reshape(col_devices, TILE, TILE)[send_order].reshape(
        row_devices, per_block, TILE, TILE
    )
    arrived = lax.all_to_all(outgoing, "row", split_axis=0, concat_axis=0, tiled=True)
    local_mask = block_of // per_block == here_row
    slot_rank = jnp.cumsum(local_mask.astype(jnp.int32), axis=1) - 1
    slot_ids = jnp.arange(per_block, dtype=jnp.int32)
    slot_pick = (
        local_mask[:, :, None] & (slot_rank[:, :, None] == slot_ids[None, None, :])
    ).astype(jnp.int32)
    row_tile = jnp.sum(parent_index[:, :, None] * slot_pick, axis=1) - here_row * row_count
    sent_to = lax.dynamic_index_in_dim(block_of, here_col, 1, keepdims=False)
    col_route = (sent_to[None, :] == jnp.arange(col_devices)[:, None]).astype(jnp.float32)
    outgoing_cols = product(col_route, arrived.reshape(row_devices, -1)).reshape(
        col_devices, per_block, TILE, TILE
    )
    arrived_cols = lax.all_to_all(outgoing_cols, "col", split_axis=0, concat_axis=0, tiled=True)
    col_match = (block_of == here_col).astype(jnp.int32)
    col_tile = parent_index - here_col * PCT
    rows_from = jnp.sum(row_tile[:, None, :] * col_match[:, :, None], axis=0)
    cols_from = jnp.sum(col_tile * col_match, axis=0)
    live_from = jnp.sum(col_match, axis=0).astype(jnp.float32)
    cols_flat = (cols_from[:, None] + jnp.zeros_like(rows_from)).reshape(-1)
    live_flat = (live_from[:, None] + jnp.zeros(rows_from.shape, jnp.float32)).reshape(-1)
    contrib = place_tiles(
        arrived_cols.reshape(-1, TILE, TILE),
        rows_from.reshape(-1),
        cols_flat,
        live_flat,
        tile_count,
    )
    contrib = (
        contrib.reshape(row_count, PCT, TILE, TILE)
        .transpose(0, 2, 1, 3)
        .reshape(row_count * TILE, PCT * TILE)
    )
    work_matrix = parent_front - contrib
    identity = jnp.eye(TILE, dtype=jnp.float32)
    owner = (here_row == 0) & (here_col == 0)
    row_tile_index = here_row * row_count + jnp.arange(row_count * TILE) // TILE
    columns = []
    for step in range(NSP):
        offset = step * TILE
        diag_tile = jnp.where(
            owner, work_matrix[offset : offset + TILE, offset : offset + TILE], identity
        )
        pivot_tile = jnp.linalg.cholesky(diag_tile)
        inverse = lax.linalg.triangular_solve(pivot_tile, identity, left_side=True, lower=True)
        pivot_pair = from_root(jnp.stack([pivot_tile, inverse]), "row", 0)
        pivot_tile = pivot_pair[0]
        inverse = pivot_pair[1]
        factored = product_rows(work_matrix[:, offset : offset + TILE], inverse)
        factored = jnp.where(row_tile_index[:, None] < step, jnp.zeros_like(factored), factored)
        current = factored[offset : offset + TILE]
        rows_panel, inverse = (
            from_root(
                factored.at[offset : offset + TILE].set(
                    jnp.where(here_row == 0, pivot_tile, current)
                ),
                "col",
                0,
            ),
            from_root(inverse, "col", 0),
        )
        source = from_root(rows_panel, "row", here_col // per_block)
        col_panel = lax.dynamic_slice_in_dim(
            source, here_col % per_block * PCT * TILE, PCT * TILE, 0
        )
        work_matrix = work_matrix - product_rows(rows_panel, col_panel)
        columns.append(rows_panel)
    return (jnp.concatenate(columns, axis=1), work_matrix)


def solution(mesh):
    placed = (P("row", "col"), P("row", "col", None), P("row", None, None), P())
    return jax.shard_map(
        per_device,
        mesh=mesh,
        in_specs=placed,
        out_specs=(P("row", None), P("row", "col")),
        check_vma=False,
    )
```

profile of v0, /device:TPU:0, one launch (start us, length us, event | category | flops | bytes accessed | tf_op | source)
XLA Modules:
  0.0 993.7 jit_solution(9929762409883196764)
XLA Ops:
  7.2 1.2 copy-done
  8.4 2.9 fusion.5
  14.3 70.5 %all-gather.2.cloned.1.call-done = f32[4096,512]{1,0:T(8,128)} async-done(((f32[256,512]{1,0:T(8,128)}), f32[4096,512]{1,0:T(8,128)}) %all-gather.2.cloned.1.call-update) | async-done | bytes 8388624 | tf_op jit(solution)/shard_map/all_gather | solution.py:52
  84.8 10.6 %fusion.69 = f32[4096,256]{1,0:T(8,128)} fusion(f32[4096,512]{1,0:T(8,128)} %all-gather.2.cloned.1.call-done, f32[256,512]{1,0:T(8,128)} %fusion.5), kind=kOutput, calls=%fused_computation.186 | convolution fusion | flops 6442450944 | bytes 13107200 | tf_op jit(solution)/shard_map/dot_general | solution.py:23
  95.4 5.0 gather_fusion
  100.4 4.8 all-to-all-start
  105.5 49.4 %all-to-all-done = f32[8,2,256,256]{3,2,1,0:T(8,128)} async-done(((f32[8,2,256,256]{3,2,1,0:T(8,128)}), f32[8,2,256,256]{3,2,1,0:T(8,128)}, u32[]{:S(2)}, u32[]{:S(2)}) %all-to-all-start) | async-done | bytes 4194336 | tf_op jit(solution)/shard_map/all_to_all | solution.py:62
  155.0 4.6 copy.52
  159.6 3.7 fusion.54
  163.3 8.1 copy.34
  171.3 5.3 all-to-all-start.1
  177.8 9.1 copy.37
  186.9 134.8 %all-to-all-done.1 = f32[16,2,256,256]{3,2,1,0:T(8,128)} async-done(((f32[16,2,256,256]{3,2,1,0:T(8,128)}), f32[16,2,256,256]{3,2,1,0:T(8,128)}, u32[]{:S(2)}, u32[]{:S(2)}) %all-to-all-start.1) | async-done | bytes 8388640 | tf_op jit(solution)/shard_map/all_to_all | solution.py:75
  321.7 17.3 %fusion.2 = f32[8,256,4,256]{3,0,1,2:T(8,128)} fusion(f32[32]{0:T(128)S(1)} %mul.78, s32[8,4]{0,1:T(4,128)S(1)} %multiply_add_fusion, s32[32]{0:T(128)S(1)} %add.154, f32[4,8,256,256]{3,2,1,0:T(8,128)} %bitcast.51), kind=kOutput, calls=%fused_computation.12 | convolution fusion | flops 805308416 | bytes 16777600 | tf_op jit(solution)/shard_map/dot_general | solution.py:17
  339.0 10.8 %copy.36 = f32[8,256,4,256]{1,0,3,2:T(8,128)} copy(f32[8,256,4,256]{3,0,1,2:T(8,128)} %fusion.2) | data formatting | bytes 16777216 | tf_op jit(solution)/shard_map/transpose | solution.py:92
  349.8 10.7 %copy.54 = f32[128,8,8,256]{3,1,2,0:T(8,128)} copy(f32[128,8,8,256]{3,2,1,0:T(8,128)} %bitcast.170) | data formatting | bytes 16777216
  360.5 11.9 %sub.79 = f32[2048,1024]{0,1:T(8,128)} subtract(f32[2048,1024]{0,1:T(8,128)} %copy.37, f32[2048,1024]{0,1:T(8,128)} %bitcast.169) | non-fusion elementwise | flops 2097152 | bytes 25165824 | tf_op jit(solution)/shard_map/sub | solution.py:95
  374.5 11.7 %cholesky.130 = f32[128,128]{1,0:T(8,128)S(1)} custom-call(f32[128,128]{1,0:T(8,128)S(1)} %cholesky.194), custom_call_target="Cholesky" | custom-call | tf_op jit(solution)/shard_map/jit(cholesky)/cholesky | solution.py:105
  386.3 10.0 %custom-call.13 = f32[1,128,128]{1,2,0:T(8,128)S(1)} custom-call(f32[1,128,128]{2,1,0:T(8,128)S(1)} %get-tuple-element.90), custom_call_target="InvertDiagBlocksLowerTriangular" | custom-call | tf_op jit(solution)/shard_map/jit(cholesky)/cholesky | solution.py:105
  396.7 11.7 %cholesky.147 = f32[128,128]{1,0:T(8,128)S(1)} custom-call(f32[128,128]{1,0:T(8,128)S(1)} %convolution_subtract_fusion.5), custom_call_target="Cholesky" | custom-call | tf_op jit(solution)/shard_map/jit(cholesky)/cholesky | solution.py:105
  410.6 4.1 while.6
  411.3 1.3 bitcast_dynamic-update-slice_fusion.4
  413.3 1.3 bitcast_dynamic-update-slice_fusion.4
  414.7 19.7 %custom-call.14 = f32[2,128,128]{1,2,0:T(8,128)S(1)} custom-call(f32[2,128,128]{2,1,0:T(8,128)S(1)} %get-tuple-element.42), custom_call_target="InvertDiagBlocksLowerTriangular" | custom-call | tf_op jit(solution)/shard_map/triangular_solve/custom-call.0 | solution.py:106
  436.3 63.0 %all-reduce.8.cloned.1.call-done = f32[2,256,256]{2,1,0:T(8,128)} async-done(((f32[2,256,256]{2,1,0:T(8,128)}), f32[2,256,256]{2,1,0:T(8,128)}) %all-reduce.8.cloned.1.call-update) | async-done | bytes 524304 | tf_op jit(solution)/shard_map/psum | solution.py:13
  499.3 5.1 convolution_select_fusion.1
  504.6 1.5 broadcast_select_fusion.3
  506.1 89.7 %all-reduce.10.cloned.1.call-done = f32[2048,256]{1,0:T(8,128)} async-done(((f32[2048,256]{1,0:T(8,128)}), f32[2048,256]{1,0:T(8,128)}) %all-reduce.10.cloned.1.call-update) | async-done | bytes 2097168 | tf_op jit(solution)/shard_map/psum | solution.py:13
  595.9 3.2 broadcast_select_fusion.2
  599.1 64.4 %all-reduce.12.cloned.1.call-done = f32[2048,256]{1,0:T(8,128)} async-done(((f32[2048,256]{1,0:T(8,128)}), f32[2048,256]{1,0:T(8,128)}) %all-reduce.12.cloned.1.call-update) | async-done | bytes 2097168 | tf_op jit(solution)/shard_map/psum | solution.py:13
  663.6 10.5 %convolution_subtract_fusion.1 = f32[2048,1024]{0,1:T(8,128)S(1)} fusion(f32[2048,1024]{0,1:T(8,128)} %sub.79, f32[2048,256]{1,0:T(8,128)S(1)} %copy-done.3, f32[2048,256]{1,0:T(8,128)} %all-reduce.12.cloned.1.call-done, s32[]{:T(128)S(6)} %select_n.189), kind=kOutput, calls=%fused_computation.10 | convolution fusion | flops 6444548096 | bytes 19922948 | tf_op jit(solution)/shard_map/dot_general | solution.py:23
  674.0 3.4 copy-done.2
  678.6 11.7 %cholesky.164 = f32[128,128]{1,0:T(8,128)S(1)} custom-call(f32[128,128]{1,0:T(8,128)S(1)} %cholesky.197), custom_call_target="Cholesky" | custom-call | tf_op jit(solution)/shard_map/jit(cholesky)/cholesky | solution.py:105
  691.0 9.8 custom-call.15
  701.3 11.7 %cholesky.181 = f32[128,128]{1,0:T(8,128)S(1)} custom-call(f32[128,128]{1,0:T(8,128)S(1)} %convolution_subtract_fusion.4), custom_call_target="Cholesky" | custom-call | tf_op jit(solution)/shard_map/jit(cholesky)/cholesky | solution.py:105
  715.2 4.1 while.7
  715.8 1.4 bitcast_dynamic-update-slice_fusion.5
  717.9 1.4 bitcast_dynamic-update-slice_fusion.5
  719.3 19.9 %custom-call.16 = f32[2,128,128]{1,2,0:T(8,128)S(1)} custom-call(f32[2,128,128]{2,1,0:T(8,128)S(1)} %get-tuple-element.43), custom_call_target="InvertDiagBlocksLowerTriangular" | custom-call | tf_op jit(solution)/shard_map/triangular_solve/custom-call.0 | solution.py:106
  741.2 60.2 %all-reduce.14.cloned.1.call-done = f32[2,256,256]{2,1,0:T(8,128)} async-done(((f32[2,256,256]{2,1,0:T(8,128)}), f32[2,256,256]{2,1,0:T(8,128)}) %all-reduce.14.cloned.1.call-update) | async-done | bytes 524304 | tf_op jit(solution)/shard_map/psum | solution.py:13
  801.5 5.1 convolution_select_fusion
  806.7 1.5 broadcast_select_fusion.1
  808.2 89.8 %all-reduce.16.cloned.1.call-done = f32[2048,256]{1,0:T(8,128)} async-done(((f32[2048,256]{1,0:T(8,128)}), f32[2048,256]{1,0:T(8,128)}) %all-reduce.16.cloned.1.call-update) | async-done | bytes 2097168 | tf_op jit(solution)/shard_map/psum | solution.py:13
  898.0 3.1 broadcast_select_fusion
  901.1 4.2 pad_maximum_fusion
  905.3 60.0 %all-reduce.18.cloned.1.call-done = f32[2048,256]{1,0:T(8,128)} async-done(((f32[2048,256]{1,0:T(8,128)}), f32[2048,256]{1,0:T(8,128)}) %all-reduce.18.cloned.1.call-update) | async-done | bytes 2097168 | tf_op jit(solution)/shard_map/psum | solution.py:13
  965.3 11.8 %convolution_subtract_fusion = f32[2048,1024]{0,1:T(8,128)} fusion(f32[2048,1024]{0,1:T(8,128)} %copy-done.2, f32[2048,256]{1,0:T(8,128)} %all-reduce.16.cloned.1.call-done, f32[2048,256]{1,0:T(8,128)} %all-reduce.18.cloned.1.call-done, s32[]{:T(128)S(6)} %select_n.189), kind=kOutput, calls=%fused_computation.9 | convolution fusion | flops 6444548096 | bytes 19922948 | tf_op jit(solution)/shard_map/dot_general | solution.py:23
  977.1 9.3 copy.44
  (100 shorter events, 17.7 us)
Async XLA Ops:
  7.2 1.2 copy-start
  7.2 77.6 %all-gather.2.cloned.1.call-start = ((), (), s32[]{:S(2)}) async-start(), calls=%async_computation.2 | async-start | bytes 8912896 | tf_op jit(solution)/shard_map/all_gather | solution.py:52
  100.4 4.9 copy-start.6
  100.4 54.5 %all-to-all-start = ((f32[8,2,256,256]{3,2,1,0:T(8,128)}), f32[8,2,256,256]{3,2,1,0:T(8,128)}, u32[]{:S(2)}, u32[]{:S(2)}) async-start(f32[8,2,256,256]{3,2,1,0:T(8,128)} %bitcast.172), calls=%async_computation | async-start | bytes 8388608 | tf_op jit(solution)/shard_map/all_to_all | solution.py:62
  171.3 150.4 %all-to-all-start.1 = ((f32[16,2,256,256]{3,2,1,0:T(8,128)}), f32[16,2,256,256]{3,2,1,0:T(8,128)}, u32[]{:S(2)}, u32[]{:S(2)}) async-start(f32[16,2,256,256]{3,2,1,0:T(8,128)} %copy.34), calls=%async_computation.1 | async-start | bytes 16777216 | tf_op jit(solution)/shard_map/all_to_all | solution.py:75
  176.7 322.7 %all-reduce.8.cloned.1.call-start = ((), (), s32[]{:S(2)}) async-start(), calls=%async_computation.3 | async-start | bytes 1048576 | tf_op jit(solution)/shard_map/psum | solution.py:13
  436.3 159.6 %all-reduce.10.cloned.1.call-start = ((), (), s32[]{:S(2)}) async-start(), calls=%async_computation.4 | async-start | bytes 4194304 | tf_op jit(solution)/shard_map/psum | solution.py:13
  499.3 5.2 copy-start.5
  506.0 157.5 %all-reduce.12.cloned.1.call-start = ((), (), s32[]{:S(2)}) async-start(), calls=%async_computation.5 | async-start | bytes 4194304 | tf_op jit(solution)/shard_map/psum | solution.py:13
  595.8 67.7 %copy-start.3 = (f32[2048,256]{1,0:T(8,128)S(1)}, f32[2048,256]{1,0:T(8,128)}, u32[]{:S(2)}) copy-start(f32[2048,256]{1,0:T(8,128)} %all-reduce.10.cloned.1.call-done) | copy-start | bytes 6291460
  599.1 202.4 %all-reduce.14.cloned.1.call-start = ((), (), s32[]{:S(2)}) async-start(), calls=%async_computation.6 | async-start | bytes 1048576 | tf_op jit(solution)/shard_map/psum | solution.py:13
  674.0 3.4 copy-start.2
  741.2 156.8 %all-reduce.16.cloned.1.call-start = ((), (), s32[]{:S(2)}) async-start(), calls=%async_computation.7 | async-start | bytes 4194304 | tf_op jit(solution)/shard_map/psum | solution.py:13
  801.5 5.2 copy-start.4
  808.2 157.1 %all-reduce.18.cloned.1.call-start = ((), (), s32[]{:S(2)}) async-start(), calls=%async_computation.8 | async-start | bytes 4194304 | tf_op jit(solution)/shard_map/psum | solution.py:13
  977.1 9.3 copy-start.1
Sparse Core Ops, SparseCore 0:
  11.4 73.3 all-gather.1
  436.4 62.9 all-reduce.7
  506.2 89.6 all-reduce.9
  599.2 64.3 all-reduce.11
  741.3 60.1 all-reduce.13
  808.3 89.6 all-reduce.15
  901.2 64.0 all-reduce.17
where the time goes:
time: 999 us; the launch traced here: 994 us
  waiting for transfers between devices  682 us (68%)
  other arithmetic  141 us (14%)
  local copies, waits for them, and re-layouts  71.9 us (7%)
  matrix products  70 us (7%)
  between operations  17.6 us (2%)
  starting transfers between devices  10.7 us (1%)
    psum x6, waiting for transfers between devices, from_root(): return lax.psum(block, axis)  427 us
    all_to_all x1, waiting for transfers between devices, per_device(): lax.all_to_all(outgoing_cols, 'col', split_axis=0, concat_axis=0, tiled=T...  135 us
    all_gather x1, waiting for transfers between devices, per_device(): lax.all_gather(own_factor, 'col', axis=0, tiled=True)  70.5 us
    another operation x13, other arithmetic, per_device(): pivot_tile = jnp.linalg.cholesky(diag_tile)  68.8 us
    all_to_all x1, waiting for transfers between devices, per_device(): lax.all_to_all(outgoing, 'row', split_axis=0, concat_axis=0, tiled=True)  49.4 us
    dot_general x6, matrix products, product_rows(): lax.dot_general(matrix_a, matrix_b, (((1,), (1,)), ((), ())), precision=l...  46 us
    another operation x3, other arithmetic, per_device(): lax.linalg.triangular_solve(pivot_tile, identity, left_side=True, lower=T...  39.6 us
    unnamed x18, local copies, waits for them, and re-layouts  38.4 us
  transfers between devices with their start and end apart: 9, of which 9 were waited for; matrix products, arithmetic and copies ran while one was open for 2% of the time, Pallas kernels for 0%

commit v1 on v0

--- a/solution.py
+++ b/solution.py
@@ -6,6 +6,11 @@
 TILE = 256
 PCT = 4
 NSP = 2
+
+
+def tiled_gather(shard, axis, dim):
+    copies = jnp.concatenate([shard] * lax.axis_size(axis), axis=dim)
+    return lax.all_to_all(copies, axis, dim, dim, tiled=True)
 
 
 def from_root(block, axis, holder):
@@ -49,7 +54,7 @@
     own_factor = product_rows(child_panels[0], child_inverses[0])
     my_list = lax.dynamic_index_in_dim(parent_index, here_row, 0, keepdims=False)
     block_of = parent_index // PCT
-    update_col = product_rows(lax.all_gather(own_factor, "col", axis=0, tiled=True), own_factor)
+    update_col = product_rows(tiled_gather(own_factor, "col", 0), own_factor)
     dest_row = my_list // PCT // per_block
     tile_ids = jnp.arange(col_devices, dtype=jnp.int32)
     same_dest = (dest_row[None, :] == dest_row[:, None]) & (tile_ids[None, :] < tile_ids[:, None])

time: 999 us -> 1090 us (1.091)
  waiting for transfers between devices: 682 us -> 758 us
  starting transfers between devices: 10.7 us -> 21.9 us
    all_to_all x0 -> x1, waiting for transfers between devices: none -> 147 us  [tiled_gather(): return lax.all_to_all(copies, axis, dim, dim, tiled=True)]
    all_gather x1 -> x0, waiting for transfers between devices: 70.5 us -> none  [per_device(): lax.all_gather(own_factor, 'col', axis=0, tiled=True)]
    unnamed x18 -> x30, local copies, waits for them, and re-layouts: 38.4 us -> 42.2 us
  transfers between devices with their start and end apart: 9 -> 9, of which waited for: 9 -> 9; matrix products, arithmetic and copies ran while one was open for 2% -> 1% of each run, Pallas kernels for 0% -> 0%
where the time goes in v1:
time: 1090 us; the launch traced here: 1080 us
  waiting for transfers between devices  758 us (70%)
  other arithmetic  141 us (13%)
  local copies, waits for them, and re-layouts  75.8 us (7%)
  matrix products  69 us (6%)
  starting transfers between devices  21.9 us (2%)
  between operations  17.7 us (2%)
    psum x6, waiting for transfers between devices, from_root(): return lax.psum(block, axis)  427 us
    all_to_all x1, waiting for transfers between devices, tiled_gather(): return lax.all_to_all(copies, axis, dim, dim, tiled=True)  147 us
    all_to_all x1, waiting for transfers between devices, per_device(): lax.all_to_all(outgoing_cols, 'col', split_axis=0, concat_axis=0, tiled=T...  135 us
    another operation x13, other arithmetic, per_device(): pivot_tile = jnp.linalg.cholesky(diag_tile)  68.8 us
    all_to_all x1, waiting for transfers between devices, per_device(): lax.all_to_all(outgoing, 'row', split_axis=0, concat_axis=0, tiled=True)  49.4 us
    dot_general x6, matrix products, product_rows(): lax.dot_general(matrix_a, matrix_b, (((1,), (1,)), ((), ())), precision=l...  45.1 us
    unnamed x30, local copies, waits for them, and re-layouts  42.2 us
    another operation x3, other arithmetic, per_device(): lax.linalg.triangular_solve(pivot_tile, identity, left_side=True, lower=T...  39.6 us
  transfers between devices with their start and end apart: 9, of which 9 were waited for; matrix products, arithmetic and copies ran while one was open for 1% of the time, Pallas kernels for 0%

profile of v1, /device:TPU:0, one launch (start us, length us, event | category | flops | bytes accessed | tf_op | source)
XLA Modules:
  0.0 1084.0 jit_solution(15797135929213506697)
XLA Ops:
  8.4 2.1 constant_dynamic-update-slice_fusion.15
  11.2 3.4 copy-done.4
  14.6 8.3 all-to-all-start
  23.8 146.7 %all-to-all-done = f32[16,256,512]{2,1,0:T(8,128)} async-done(((f32[16,256,512]{2,1,0:T(8,128)}), f32[16,256,512]{2,1,0:T(8,128)}, u32[]{:S(2)}, u32[]{:S(2)}) %all-to-all-start) | async-done | bytes 8388640 | tf_op jit(solution)/shard_map/all_to_all | solution.py:13
  170.6 10.5 fusion.9
  181.1 5.0 gather_fusion
  186.1 4.7 all-to-all-start.1
  191.0 49.4 %all-to-all-done.1 = f32[8,2,256,256]{3,2,1,0:T(8,128)} async-done(((f32[8,2,256,256]{3,2,1,0:T(8,128)}), f32[8,2,256,256]{3,2,1,0:T(8,128)}, u32[]{:S(2)}, u32[]{:S(2)}) %all-to-all-start.1) | async-done | bytes 4194336 | tf_op jit(solution)/shard_map/all_to_all | solution.py:67
  240.5 4.6 copy.52
  245.1 3.7 fusion.56
  248.8 8.1 copy.34
  256.8 8.4 all-to-all-start.2
  266.3 9.1 copy.37
  275.5 134.8 %all-to-all-done.2 = f32[16,2,256,256]{3,2,1,0:T(8,128)} async-done(((f32[16,2,256,256]{3,2,1,0:T(8,128)}), f32[16,2,256,256]{3,2,1,0:T(8,128)}, u32[]{:S(2)}, u32[]{:S(2)}) %all-to-all-start.2) | async-done | bytes 8388640 | tf_op jit(solution)/shard_map/all_to_all | solution.py:80
  410.3 17.3 %fusion.2 = f32[8,256,4,256]{3,0,1,2:T(8,128)} fusion(f32[32]{0:T(128)S(1)} %mul.78, s32[8,4]{0,1:T(4,128)S(1)} %multiply_add_fusion, s32[32]{0:T(128)S(1)} %add.154, f32[4,8,256,256]{3,2,1,0:T(8,128)} %bitcast.52), kind=kOutput, calls=%fused_computation.12 | convolution fusion | flops 805308416 | bytes 16777600 | tf_op jit(solution)/shard_map/dot_general | solution.py:22
  427.6 10.8 copy.36
  438.4 10.7 copy.54
  449.1 11.9 %sub.79 = f32[2048,1024]{0,1:T(8,128)} subtract(f32[2048,1024]{0,1:T(8,128)} %copy.37, f32[2048,1024]{0,1:T(8,128)} %bitcast.174) | non-fusion elementwise | flops 2097152 | bytes 25165824 | tf_op jit(solution)/shard_map/sub | solution.py:100
  463.1 11.7 %cholesky.130 = f32[128,128]{1,0:T(8,128)S(1)} custom-call(f32[128,128]{1,0:T(8,128)S(1)} %cholesky.194), custom_call_target="Cholesky" | custom-call | tf_op jit(solution)/shard_map/jit(cholesky)/cholesky | solution.py:110
  474.8 10.0 custom-call.13
  485.3 11.7 %cholesky.147 = f32[128,128]{1,0:T(8,128)S(1)} custom-call(f32[128,128]{1,0:T(8,128)S(1)} %convolution_subtract_fusion.5), custom_call_target="Cholesky" | custom-call | tf_op jit(solution)/shard_map/jit(cholesky)/cholesky | solution.py:110
  499.1 4.1 while.6
  499.8 1.3 bitcast_dynamic-update-slice_fusion.4
  503.2 19.7 %custom-call.14 = f32[2,128,128]{1,2,0:T(8,128)S(1)} custom-call(f32[2,128,128]{2,1,0:T(8,128)S(1)} %get-tuple-element.42), custom_call_target="InvertDiagBlocksLowerTriangular" | custom-call | tf_op jit(solution)/shard_map/triangular_solve/custom-call.0 | solution.py:111
  524.9 63.0 %all-reduce.8.cloned.1.call-done = f32[2,256,256]{2,1,0:T(8,128)} async-done(((f32[2,256,256]{2,1,0:T(8,128)}), f32[2,256,256]{2,1,0:T(8,128)}) %all-reduce.8.cloned.1.call-update) | async-done | bytes 524304 | tf_op jit(solution)/shard_map/psum | solution.py:18
  587.9 5.1 convolution_select_fusion.1
  594.0 1.5 broadcast_select_fusion.3
  595.5 89.7 %all-reduce.10.cloned.1.call-done = f32[2048,256]{1,0:T(8,128)} async-done(((f32[2048,256]{1,0:T(8,128)}), f32[2048,256]{1,0:T(8,128)}) %all-reduce.10.cloned.1.call-update) | async-done | bytes 2097168 | tf_op jit(solution)/shard_map/psum | solution.py:18
  685.3 3.2 broadcast_select_fusion.2
  688.6 64.6 %all-reduce.12.cloned.1.call-done = f32[2048,256]{1,0:T(8,128)} async-done(((f32[2048,256]{1,0:T(8,128)}), f32[2048,256]{1,0:T(8,128)}) %all-reduce.12.cloned.1.call-update) | async-done | bytes 2097168 | tf_op jit(solution)/shard_map/psum | solution.py:18
  753.1 10.5 convolution_subtract_fusion.1
  763.6 3.4 copy-done.2
  768.2 11.7 %cholesky.164 = f32[128,128]{1,0:T(8,128)S(1)} custom-call(f32[128,128]{1,0:T(8,128)S(1)} %cholesky.197), custom_call_target="Cholesky" | custom-call | tf_op jit(solution)/shard_map/jit(cholesky)/cholesky | solution.py:110
  780.0 9.8 custom-call.15
  790.2 11.7 %cholesky.181 = f32[128,128]{1,0:T(8,128)S(1)} custom-call(f32[128,128]{1,0:T(8,128)S(1)} %convolution_subtract_fusion.4), custom_call_target="Cholesky" | custom-call | tf_op jit(solution)/shard_map/jit(cholesky)/cholesky | solution.py:110
  804.8 4.1 while.7
  805.4 1.4 bitcast_dynamic-update-slice_fusion.5
  807.4 1.4 bitcast_dynamic-update-slice_fusion.5
  808.9 19.9 %custom-call.16 = f32[2,128,128]{1,2,0:T(8,128)S(1)} custom-call(f32[2,128,128]{2,1,0:T(8,128)S(1)} %get-tuple-element.43), custom_call_target="InvertDiagBlocksLowerTriangular" | custom-call | tf_op jit(solution)/shard_map/triangular_solve/custom-call.0 | solution.py:111
  830.8 60.3 %all-reduce.14.cloned.1.call-done = f32[2,256,256]{2,1,0:T(8,128)} async-done(((f32[2,256,256]{2,1,0:T(8,128)}), f32[2,256,256]{2,1,0:T(8,128)}) %all-reduce.14.cloned.1.call-update) | async-done | bytes 524304 | tf_op jit(solution)/shard_map/psum | solution.py:18
  891.1 5.1 convolution_select_fusion
  897.2 1.5 broadcast_select_fusion.1
  898.7 89.8 %all-reduce.16.cloned.1.call-done = f32[2048,256]{1,0:T(8,128)} async-done(((f32[2048,256]{1,0:T(8,128)}), f32[2048,256]{1,0:T(8,128)}) %all-reduce.16.cloned.1.call-update) | async-done | bytes 2097168 | tf_op jit(solution)/shard_map/psum | solution.py:18
  988.4 3.1 broadcast_select_fusion
  991.5 4.2 pad_maximum_fusion
  995.7 59.9 %all-reduce.18.cloned.1.call-done = f32[2048,256]{1,0:T(8,128)} async-done(((f32[2048,256]{1,0:T(8,128)}), f32[2048,256]{1,0:T(8,128)}) %all-reduce.18.cloned.1.call-update) | async-done | bytes 2097168 | tf_op jit(solution)/shard_map/psum | solution.py:18
  1055.6 11.9 %convolution_subtract_fusion = f32[2048,1024]{0,1:T(8,128)} fusion(f32[2048,1024]{0,1:T(8,128)} %copy-done.2, f32[2048,256]{1,0:T(8,128)} %all-reduce.16.cloned.1.call-done, f32[2048,256]{1,0:T(8,128)} %all-reduce.18.cloned.1.call-done, s32[]{:T(128)S(6)} %select_n.189), kind=kOutput, calls=%fused_computation.9 | convolution fusion | flops 6444548096 | bytes 19922948 | tf_op jit(solution)/shard_map/dot_general | solution.py:28
  1067.5 9.2 copy.44
  (112 shorter events, 20.5 us)
Async XLA Ops:
  7.2 1.2 copy-start
  11.2 3.4 copy-start.4
  14.6 8.3 copy-start.5
  14.6 156.0 %all-to-all-start = ((f32[16,256,512]{2,1,0:T(8,128)}), f32[16,256,512]{2,1,0:T(8,128)}, u32[]{:S(2)}, u32[]{:S(2)}) async-start(f32[16,256,512]{2,1,0:T(8,128)} %bitcast.178), calls=%async_computation | async-start | bytes 16777216 | tf_op jit(solution)/shard_map/all_to_all | solution.py:13
  186.1 54.4 %all-to-all-start.1 = ((f32[8,2,256,256]{3,2,1,0:T(8,128)}), f32[8,2,256,256]{3,2,1,0:T(8,128)}, u32[]{:S(2)}, u32[]{:S(2)}) async-start(f32[8,2,256,256]{3,2,1,0:T(8,128)} %bitcast.176), calls=%async_computation.1 | async-start | bytes 8388608 | tf_op jit(solution)/shard_map/all_to_all | solution.py:67
  256.8 153.4 %all-to-all-start.2 = ((f32[16,2,256,256]{3,2,1,0:T(8,128)}), f32[16,2,256,256]{3,2,1,0:T(8,128)}, u32[]{:S(2)}, u32[]{:S(2)}) async-start(f32[16,2,256,256]{3,2,1,0:T(8,128)} %copy.34), calls=%async_computation.2 | async-start | bytes 16777216 | tf_op jit(solution)/shard_map/all_to_all | solution.py:80
  265.2 322.7 %all-reduce.8.cloned.1.call-start = ((), (), s32[]{:S(2)}) async-start(), calls=%async_computation.3 | async-start | bytes 1048576 | tf_op jit(solution)/shard_map/psum | solution.py:18
  524.8 160.5 %all-reduce.10.cloned.1.call-start = ((), (), s32[]{:S(2)}) async-start(), calls=%async_computation.4 | async-start | bytes 4194304 | tf_op jit(solution)/shard_map/psum | solution.py:18
  595.5 157.7 %all-reduce.12.cloned.1.call-start = ((), (), s32[]{:S(2)}) async-start(), calls=%async_computation.5 | async-start | bytes 4194304 | tf_op jit(solution)/shard_map/psum | solution.py:18
  685.3 67.9 %copy-start.3 = (f32[2048,256]{1,0:T(8,128)S(1)}, f32[2048,256]{1,0:T(8,128)}, u32[]{:S(2)}) copy-start(f32[2048,256]{1,0:T(8,128)} %all-reduce.10.cloned.1.call-done) | copy-start | bytes 6291460
  688.5 202.6 %all-reduce.14.cloned.1.call-start = ((), (), s32[]{:S(2)}) async-start(), calls=%async_computation.6 | async-start | bytes 1048576 | tf_op jit(solution)/shard_map/psum | solution.py:18
  763.6 3.4 copy-start.2
  830.7 157.7 %all-reduce.16.cloned.1.call-start = ((), (), s32[]{:S(2)}) async-start(), calls=%async_computation.7 | async-start | bytes 4194304 | tf_op jit(solution)/shard_map/psum | solution.py:18
  898.6 156.9 %all-reduce.18.cloned.1.call-start = ((), (), s32[]{:S(2)}) async-start(), calls=%async_computation.8 | async-start | bytes 4194304 | tf_op jit(solution)/shard_map/psum | solution.py:18
  1055.6 21.1 %copy-start.1 = (f32[1,512,512]{2,1,0:T(8,128)S(1)}, f32[1,512,512]{2,1,0:T(8,128)}, u32[]{:S(2)}) copy-start(f32[1,512,512]{2,1,0:T(8,128)} %param.13) | copy-start | bytes 3145732
Sparse Core Ops, SparseCore 0:
  524.9 62.9 all-reduce.7
  595.6 89.6 all-reduce.9
  688.6 64.4 all-reduce.11
  830.8 60.1 all-reduce.13
  898.8 89.6 all-reduce.15
  991.7 63.8 all-reduce.17
